TPU v7x, 256 devices: a whole 4x4x8 slice. The times are simulated.
256 devices in a mesh: head: 8 (over y, core), doc: 32 (over x, z).
Axes of the slice: x: 4, y: 4, z: 8, core: 2. Of those that a mesh axis runs over, the one named last changes fastest.
Arguments:
- tokens: bfloat16 [12288, 1024], P('doc'), may hold values from -6 to 6
- w_qkv: bfloat16 [1024, 3, 1024], P(None, None, 'head'), may hold values from -0.1875 to 0.1875
- w_out: bfloat16 [1024, 1024], P('head'), may hold values from -0.1875 to 0.1875
- w_up: bfloat16 [1024, 4096], P(None, 'head'), may hold values from -0.1875 to 0.1875
- w_down: bfloat16 [4096, 1024], P('head'), may hold values from -0.09375 to 0.09375
- gain_one: float32 [1024], replicated, may hold values from 0.5 to 1.5
- gain_two: float32 [1024], replicated, may hold values from 0.5 to 1.5
- rel_table: bfloat16 [512, 1024], replicated, may hold values from -6 to 6
- prompt_cache: bfloat16 [2, 4096, 1024], P(None, 'doc', 'head'), may hold values from -480 to 480
- w_proj: bfloat16 [1024, 128], replicated, may hold values from -0.1875 to 0.1875
- doc_vectors: bfloat16 [2048, 256, 128], P('doc'), may hold values from -0.5 to 0.5
- doc_lengths: int32 [2048], P('doc'), may hold values from 8 to 256, as said below
- group_ids: int32 [384], P('doc'), may hold values from 0 to 63
- candidates: int32 [384, 64], P('doc', 'head'), may hold values from 0 to 2047, as said below
Outputs:
- query_vectors: bfloat16 [12288, 128], P('doc')
- scores: float32 [384, 64], P('doc', 'head')
Inputs may be any that keep to these rules, and one draw needn't show every extreme that they name: Split candidates into aligned blocks of 12 requests by 8 columns (one index of doc with one of head). Index o of doc holds documents o * 64 to o * 64 + 63. In each block at most 6 entries name documents held by one index of doc, and one index of doc, the same for all blocks, is named by exactly 6 entries of every block. The documents named within one block are distinct. Some document has exactly 256 tokens; token slots from doc_lengths on are padding.
All inputs are finite; a program needn't handle non-finite values.
Results may differ from a plain program's by a relative error of at most 0.02.
Values may be sent and summed in bfloat16 or wider, within the bound.
A program may use at most 128 MiB of HBM per device.

v0:
```python
import math
import jax
import jax.numpy as jnp
from jax import lax
from jax.sharding import PartitionSpec as P

HD = 64
RELS = 512
QLEN = 32
PLEN = 64
DOC_DEV = 64


def layer_norm(values, gain):
    centre = values - jnp.mean(values, axis=-1, keepdims=True)
    spread = jnp.mean(centre * centre, axis=-1, keepdims=True)
    return centre * lax.rsqrt(spread + 1e-07) * gain


def slot_order(holders):
    count = holders.shape[0]
    same = holders[:, None] == holders[None, :]
    earlier = jnp.arange(count)[:, None] > jnp.arange(count)[None, :]
    return jnp.sum(same & earlier, axis=1)


def rate_slots(slot_query, slot_doc, doc_vectors, doc_lengths):
    shape = slot_doc.shape
    flat_doc = slot_doc.reshape(-1)
    flat_query = slot_query.reshape((flat_doc.shape[0],) + slot_query.shape[-2:])
    safe_doc = jnp.maximum(flat_doc, 0)
    documents = doc_vectors[safe_doc]
    lengths = doc_lengths[safe_doc]
    sims = jnp.einsum("sqe,sje->sqj", flat_query, documents, preferred_element_type=jnp.float32)
    live = jnp.arange(documents.shape[1], dtype=jnp.int32)[None, None, :] < lengths[:, None, None]
    best = jnp.max(jnp.where(live, sims, -jnp.inf), axis=2)
    totals = jnp.where(flat_doc >= 0, jnp.sum(best, axis=1), 0.0)
    return totals.reshape(shape)


def body(
    tokens,
    w_qkv,
    w_out,
    w_up,
    w_down,
    gain_one,
    gain_two,
    rel_table,
    prompt_cache,
    w_proj,
    doc_vectors,
    doc_lengths,
    group_ids,
    candidates,
):
    rows_dev = tokens.shape[0]
    req_dev = rows_dev // QLEN
    width = w_qkv.shape[2]
    heads_loc = width // HD
    half = RELS // 2
    scale_root = math.sqrt(3 * HD)
    gathered = lax.all_gather(prompt_cache, "doc", axis=1, tiled=True)
    weights_split = w_qkv.reshape(w_qkv.shape[0], 3, heads_loc, HD)
    projected_all = jnp.einsum(
        "td,dchf->chtf", tokens, weights_split, preferred_element_type=jnp.float32
    ).astype(jnp.bfloat16)
    rel_both = jnp.einsum(
        "rd,dchf->chrf", rel_table, weights_split[:, :2], preferred_element_type=jnp.float32
    ).astype(jnp.bfloat16)
    head_shape = (heads_loc, req_dev, QLEN, HD)
    query_four = projected_all[0].reshape(head_shape)
    keys_four = projected_all[1].reshape(head_shape)
    values_four = projected_all[2].reshape(head_shape)
    groups_all = gathered.shape[1] // PLEN
    cache_all = gathered.reshape(2, groups_all, PLEN, heads_loc, HD)
    picked = jnp.transpose(cache_all[:, group_ids], (0, 3, 1, 2, 4))
    keys = jnp.concatenate([keys_four, picked[0]], axis=2)
    values = jnp.concatenate([values_four, picked[1]], axis=2)
    pos_query = PLEN + jnp.arange(QLEN, dtype=jnp.int32)
    pos_key = jnp.concatenate([pos_query, jnp.arange(PLEN, dtype=jnp.int32)])
    index_one = pos_query[:, None] - pos_key[None, :] + half
    index_two = pos_key[:, None] - pos_query[None, :] + half
    rel_k_rows = rel_both[1][:, index_one]
    rel_q_rows = rel_both[0][:, index_two]
    c2p = jnp.einsum("hrqd,hqkd->hrqk", query_four, rel_k_rows, preferred_element_type=jnp.float32)
    p2c = jnp.einsum("hrkd,hkqd->hrqk", keys, rel_q_rows, preferred_element_type=jnp.float32)
    content = jnp.einsum("hrqd,hrkd->hrqk", query_four, keys, preferred_element_type=jnp.float32)
    logits = (content + c2p + p2c) / scale_root
    largest = jnp.max(logits, axis=-1, keepdims=True)
    weights = jnp.exp(logits - largest)
    denominator = jnp.sum(weights, axis=-1)
    summed = jnp.einsum(
        "hrqk,hrkd->hrqd", weights.astype(jnp.bfloat16), values, preferred_element_type=jnp.float32
    )
    attended = (summed / denominator[..., None]).astype(jnp.bfloat16)
    out_split = w_out.reshape(heads_loc, HD, w_out.shape[1])
    attn_part = jnp.einsum(
        "hrqd,hde->rqe", attended, out_split, preferred_element_type=jnp.float32
    ).reshape(rows_dev, w_out.shape[1])
    attn_total = lax.psum(attn_part.astype(jnp.bfloat16), "head").astype(jnp.float32)
    hidden_one = layer_norm(tokens.astype(jnp.float32) + attn_total, gain_one).astype(jnp.bfloat16)
    inner = jax.nn.gelu(
        jnp.dot(hidden_one, w_up, preferred_element_type=jnp.float32), approximate=False
    ).astype(jnp.bfloat16)
    ffn_total = lax.psum(
        jnp.dot(inner, w_down, preferred_element_type=jnp.float32).astype(jnp.bfloat16), "head"
    ).astype(jnp.float32)
    hidden_two = layer_norm(hidden_one.astype(jnp.float32) + ffn_total, gain_two).astype(
        jnp.bfloat16
    )
    projected = jnp.dot(hidden_two, w_proj, preferred_element_type=jnp.float32)
    query_vectors = (
        projected * lax.rsqrt(jnp.sum(projected * projected, axis=-1, keepdims=True) + 1e-06)
    ).astype(jnp.bfloat16)
    shards = lax.axis_size("doc")
    cand_dev = candidates.shape[1]
    pairs = req_dev * cand_dev
    capacity = max(2, 2 * pairs // shards)
    flat_cand = candidates.reshape(-1)
    holders = flat_cand // DOC_DEV
    request_of = jnp.arange(pairs, dtype=jnp.int32) // cand_dev
    slot_rank = slot_order(holders)
    copies, cand_copies = (
        lax.all_gather(query_vectors, "doc", axis=0, tiled=True),
        lax.all_gather(candidates, "doc", axis=0, tiled=True),
    )
    all_query = copies.reshape(shards, req_dev, QLEN, copies.shape[1])
    all_cand = cand_copies.reshape(shards, pairs)
    holder_all = all_cand // DOC_DEV
    local_all = all_cand % DOC_DEV
    rank_all = jax.vmap(slot_order)(holder_all)
    own_index = lax.axis_index("doc")
    chosen = (holder_all[:, None, :] == own_index) & (
        rank_all[:, None, :] == jnp.arange(capacity, dtype=jnp.int32)[None, :, None]
    )
    filled = jnp.any(chosen, axis=2)
    slot_request = jnp.sum(jnp.where(chosen, request_of[None, None, :], 0), axis=2)
    slot_doc = jnp.where(
        filled, jnp.sum(jnp.where(chosen, local_all[:, None, :], 0), axis=2), -1
    ).astype(jnp.int32)
    slot_query = all_query[jnp.arange(shards)[:, None], slot_request]
    slot_scores = rate_slots(slot_query, slot_doc, doc_vectors, doc_lengths)
    returned = lax.all_to_all(slot_scores, "doc", split_axis=0, concat_axis=0, tiled=True)
    scores = returned.reshape(-1)[holders * capacity + slot_rank].reshape(candidates.shape)
    return (query_vectors, scores)


def solution(mesh):
    placed = (
        P("doc", None),
        P(None, None, "head"),
        P("head", None),
        P(None, "head"),
        P("head", None),
        P(),
        P(),
        P(),
        P(None, "doc", "head"),
        P(),
        P("doc", None, None),
        P("doc"),
        P("doc"),
        P("doc", "head"),
    )
    return jax.shard_map(
        body,
        mesh=mesh,
        in_specs=placed,
        out_specs=(P("doc", None), P("doc", "head")),
        check_vma=False,
    )
```

profile of v0, /device:TPU:8, one launch (start us, length us, event | category | flops | bytes accessed | tf_op | source)
XLA Modules:
  0.0 386.3 jit_solution(13940295378734445451)
XLA Ops:
  8.2 1.4 copy.182
  10.4 20.3 %gather_fusion.2 = bf16[3072,2,64]{2,1,0:T(2,128)(2,1)} fusion(bf16[2,512,64]{2,0,1:T(2,128)(2,1)S(1)} %copy.193, s32[3072]{0:T(1024)S(1)} %broadcast_clamp_fusion), kind=kCustom, calls=%fused_computation.2 | custom fusion | bytes 1585152 | tf_op jit(solution)/shard_map/gather | solution.py:85
  30.6 2.9 copy.194
  35.6 20.3 %gather_fusion.1 = bf16[3072,2,64]{2,1,0:T(2,128)(2,1)} fusion(bf16[2,512,64]{2,0,1:T(2,128)(2,1)S(1)} %copy.189, s32[3072]{0:T(1024)S(1)} %broadcast_clamp_fusion.1), kind=kCustom, calls=%fused_computation.1 | custom fusion | bytes 1585152 | tf_op jit(solution)/shard_map/gather | solution.py:84
  55.9 4.0 %copy.190 = bf16[32,96,2,64]{1,3,0,2:T(8,128)(2,1)S(1)} copy(bf16[32,96,2,64]{3,2,1,0:T(2,128)(2,1)} %bitcast.83) | data formatting | bytes 1572864 | tf_op jit(solution)/shard_map/gather | solution.py:84
  61.0 1.7 copy.197
  62.7 1.9 copy.198
  64.6 1.2 fusion.11
  65.7 25.8 %all-gather.4.cloned.1.call-done = bf16[2,4096,128]{2,1,0:T(8,128)(2,1)} async-done(((bf16[2,128,128]{2,1,0:T(8,128)(2,1)}), bf16[2,4096,128]{2,1,0:T(8,128)(2,1)}) %all-gather.4.cloned.1.call-update) | async-done | bytes 2097168 | tf_op jit(solution)/shard_map/all_gather | solution.py:63
  91.5 8.2 %reshape.599 = bf16[2,64,64,2,64]{4,3,2,1,0:T(2,128)(2,1)} reshape(bf16[2,4096,128]{2,1,0:T(8,128)(2,1)} %all-gather.4.cloned.1.call-done) | data formatting | bytes 4194304 | tf_op jit(solution)/shard_map/reshape | solution.py:76
  99.7 5.4 %copy.186 = bf16[2,64,64,2,64]{4,2,3,1,0:T(8,128)(2,1)} copy(bf16[2,64,64,2,64]{4,3,2,1,0:T(2,128)(2,1)} %reshape.599) | data formatting | bytes 4194304 | tf_op jit(solution)/shard_map/reshape | solution.py:76
  105.2 3.7 gather_fusion
  108.9 1.5 copy.187
  112.1 3.5 fusion.107
  115.6 1.9 copy.196
  119.0 1.3 bitcast_convert_fusion
  120.6 61.6 %all-reduce.3.cloned.1.call-done = bf16[384,1024]{1,0:T(8,128)(2,1)} async-done(((bf16[384,1024]{1,0:T(8,128)(2,1)}), bf16[384,1024]{1,0:T(8,128)(2,1)}) %all-reduce.3.cloned.1.call-update) | async-done | bytes 786448 | tf_op jit(solution)/shard_map/psum | solution.py:101
  182.2 1.5 fusion.1
  184.5 4.8 %convolution_convert_fusion = bf16[384,1024]{1,0:T(8,128)(2,1)} fusion(bf16[512,1024]{1,0:T(8,128)(2,1)S(1)} %copy-done, bf16[384,1024]{1,0:T(8,128)(2,1)S(1)} %multiply_convert_fusion.1, bf16[1024,512]{1,0:T(8,128)(2,1)} %param.17), kind=kOutput, calls=%fused_computation.20 | convolution fusion | flops 818479104 | bytes 3670016 | tf_op jit(solution)/shard_map/dot_general | solution.py:107
  189.4 66.1 %all-reduce.5.cloned.1.call-done = bf16[384,1024]{1,0:T(8,128)(2,1)} async-done(((bf16[384,1024]{1,0:T(8,128)(2,1)}), bf16[384,1024]{1,0:T(8,128)(2,1)}) %all-reduce.5.cloned.1.call-update) | async-done | bytes 786448 | tf_op jit(solution)/shard_map/psum | solution.py:106
  255.5 1.5 fusion.3
  259.0 44.2 %all-gather = s32[32,12,8]{1,2,0:T(8,128)S(1)} all-gather(s32[1,12,8]{1,2,0:T(8,128)S(1)} %bitcast.95), channel_id=1, replica_groups=mesh['head'=8,'doc'=32] {'doc'}, dimensions={0}, use_global_device_ids=true | all-gather | bytes 12672 | tf_op jit(solution)/shard_map/all_gather | solution.py:126
  303.4 1.2 convert_reduce_fusion
  305.6 10.3 %gather_fusion.5 = bf16[192,256,128]{2,1,0:T(8,128)(2,1)} fusion(bf16[64,256,128]{2,1,0:T(8,128)(2,1)} %param.24, s32[1024]{0:T(1024)S(1)} %pad_clamp_fusion.1), kind=kCustom, calls=%fused_computation.5 | custom fusion | bytes 25166592 | tf_op jit(solution)/shard_map/gather | solution.py:32
  315.8 1.5 gather_fusion.3
  317.7 21.3 %all-gather.6.cloned.1.call-done = bf16[12288,128]{0,1:T(8,128)(2,1)} async-done(((bf16[384,128]{0,1:T(8,128)(2,1)}), bf16[12288,128]{0,1:T(8,128)(2,1)}) %all-gather.6.cloned.1.call-update) | async-done | bytes 3145744 | tf_op jit(solution)/shard_map/all_gather | solution.py:125
  339.0 4.7 %copy.206 = bf16[12288,128]{1,0:T(8,128)(2,1)} copy(bf16[12288,128]{0,1:T(8,128)(2,1)} %all-gather.6.cloned.1.call-done) | data formatting | bytes 6291456 | tf_op jit(solution)/shard_map/all_gather | solution.py:125
  343.8 3.7 gather_fusion.4
  347.5 9.2 %select_reduce_fusion = f32[192,32]{1,0:T(8,128)S(1)} fusion(pred[192,256]{1,0:T(8,128)(4,1)S(1)} %iota_compare_fusion, bf16[192,32,128]{2,1,0:T(8,128)(2,1)S(1)} %gather_fusion.4, bf16[192,256,128]{2,1,0:T(8,128)(2,1)} %gather_fusion.5), kind=kOutput, calls=%fused_computation.7 | convolution fusion | flops 405792768 | bytes 14229504 | tf_op jit(solution)/shard_map/sqe,sje->sqj/dot_general | solution.py:34
  357.6 9.0 %all-to-all-start = ((f32[32,1,6]{2,1,0:T(1,128)}), f32[32,1,6]{2,1,0:T(1,128)S(1)}, u32[]{:S(2)}, u32[]{:S(2)}) async-start(f32[32,1,6]{2,1,0:T(1,128)} %copy.210), calls=%async_computation | async-start | bytes 32768 | tf_op jit(solution)/shard_map/all_to_all | solution.py:144
  367.5 9.0 %all-to-all-done = f32[32,1,6]{2,1,0:T(1,128)S(1)} async-done(((f32[32,1,6]{2,1,0:T(1,128)}), f32[32,1,6]{2,1,0:T(1,128)S(1)}, u32[]{:S(2)}, u32[]{:S(2)}) %all-to-all-start) | async-done | bytes 800 | tf_op jit(solution)/shard_map/all_to_all | solution.py:144
  377.8 1.3 gather_fusion.6
  (110 shorter events, 16.2 us)
Async XLA Ops:
  7.2 177.3 %copy-start = (bf16[512,1024]{1,0:T(8,128)(2,1)S(1)}, bf16[512,1024]{1,0:T(8,128)(2,1)}, u32[]{:S(2)}) copy-start(bf16[512,1024]{1,0:T(8,128)(2,1)} %param.18) | copy-start | bytes 3145732
  7.2 2.5 copy-start.6
  7.2 84.3 %all-gather.4.cloned.1.call-start = ((), (), s32[]{:S(2)}) async-start(), calls=%async_computation.1 | async-start | bytes 2162688 | tf_op jit(solution)/shard_map/all_gather | solution.py:63
  7.9 174.3 %all-reduce.3.cloned.1.call-start = ((), (), s32[]{:S(2)}) async-start(), calls=%async_computation.2 | async-start | bytes 1572864 | tf_op jit(solution)/shard_map/psum | solution.py:101
  30.6 2.9 copy-start.2
  55.9 8.7 %copy-start.15 = (s32[12]{0:T(128)S(1)}, s32[12]{0:T(128)}, u32[]{:S(2)}) copy-start(s32[12]{0:T(128)} %param.26) | copy-start | bytes 148
  115.6 1.9 copy-start.5
  117.5 1.0 copy-start.8
  117.5 1.1 copy-start.9
  117.8 1.2 copy-start.10
  120.4 63.8 %copy-start.12 = (f32[1024]{0:T(1024)S(1)}, f32[1024]{0:T(1024)}, u32[]{:S(2)}) copy-start(f32[1024]{0:T(1024)} %param.19) | copy-start | bytes 12292
  120.4 135.2 %all-reduce.5.cloned.1.call-start = ((), (), s32[]{:S(2)}) async-start(), calls=%async_computation.3 | async-start | bytes 1572864 | tf_op jit(solution)/shard_map/psum | solution.py:106
  182.2 1.5 copy-start.3
  189.4 68.1 %copy-start.13 = (bf16[1024,128]{1,0:T(8,128)(2,1)S(1)}, bf16[1024,128]{1,0:T(8,128)(2,1)}, u32[]{:S(2)}) copy-start(bf16[1024,128]{1,0:T(8,128)(2,1)} %param.23) | copy-start | bytes 786436
  189.4 68.1 %copy-start.14 = (f32[1024]{0:T(1024)S(1)}, f32[1024]{0:T(1024)}, u32[]{:S(2)}) copy-start(f32[1024]{0:T(1024)} %param.20) | copy-start | bytes 12292
  189.4 149.7 %all-gather.6.cloned.1.call-start = ((), (), s32[]{:S(2)}) async-start(), calls=%async_computation.4 | async-start | bytes 3244032 | tf_op jit(solution)/shard_map/all_gather | solution.py:125
  255.5 1.5 copy-start.4
  257.4 1.3 copy-start.11
  305.5 10.3 %copy-start.1 = (s32[64]{0:T(128)S(1)}, s32[64]{0:T(128)}, u32[]{:S(2)}) copy-start(s32[64]{0:T(128)} %param.25) | copy-start | bytes 772
  347.5 19.2 %copy-start.7 = (bf16[384,128]{0,1:T(8,128)(2,1)S(1)}, bf16[384,128]{0,1:T(8,128)(2,1)}, u32[]{:S(2)}) copy-start(bf16[384,128]{0,1:T(8,128)(2,1)} %multiply_convert_fusion.3) | copy-start | bytes 294916
  357.6 18.8 %all-to-all-start = ((f32[32,1,6]{2,1,0:T(1,128)}), f32[32,1,6]{2,1,0:T(1,128)S(1)}, u32[]{:S(2)}, u32[]{:S(2)}) async-start(f32[32,1,6]{2,1,0:T(1,128)} %copy.210), calls=%async_computation | async-start | bytes 32768 | tf_op jit(solution)/shard_map/all_to_all | solution.py:144
Sparse Core Ops, SparseCore 0:
  10.6 80.8 all-gather.3
  120.5 61.6 all-reduce.2
  189.5 65.9 all-reduce.4
  258.9 80.1 all-gather.5
where the time goes:
time: 387 us; the launch traced here: 386 us
  waiting for transfers between devices  185 us (48%)
  local copies, waits for them, and re-layouts  103 us (27%)
  blocking collectives  44.2 us (11%)
  matrix products  22.4 us (6%)
  between operations  14.2 us (4%)
  starting transfers between devices  9.37 us (2%)
  other arithmetic  8.49 us (2%)
    psum x1, waiting for transfers between devices, body(): lax.psum(jnp.dot(inner, w_down, preferred_element_type=jnp.float32).astyp...  66.1 us
    psum x1, waiting for transfers between devices, body(): lax.psum(attn_part.astype(jnp.bfloat16), 'head').astype(jnp.float32)  61.6 us
    all_gather x1, blocking collectives, body(): lax.all_gather(candidates, 'doc', axis=0, tiled=True)  44.2 us
    all_gather x1, waiting for transfers between devices, body(): gathered = lax.all_gather(prompt_cache, 'doc', axis=1, tiled=True)  25.8 us
    gather x2, local copies, waits for them, and re-layouts, body(): rel_k_rows = rel_both[1][:, index_one]  24.3 us
    gather x2, local copies, waits for them, and re-layouts, body(): rel_q_rows = rel_both[0][:, index_two]  23.2 us
    all_gather x1, waiting for transfers between devices, body(): lax.all_gather(query_vectors, 'doc', axis=0, tiled=True)  21.3 us
    reshape x2, local copies, waits for them, and re-layouts, body(): cache_all = gathered.reshape(2, groups_all, PLEN, heads_loc, HD)  13.7 us
  transfers between devices with their start and end apart: 5, of which 5 were waited for; matrix products, arithmetic and copies ran while one was open for 19% of the time, Pallas kernels for 0%

commit v1 on v0

--- a/solution.py
+++ b/solution.py
@@ -1,3 +1,4 @@
+import functools
 import math
 import jax
 import jax.numpy as jnp
@@ -9,6 +10,14 @@
 QLEN = 32
 PLEN = 64
 DOC_DEV = 64
+
+
+def expand_quarters_on(here_x, bus_axis):
+    z1 = lax.all_gather(here_x, axis_name=bus_axis)
+    return jnp.sum(z1, axis=0)
+
+
+solve_inputs = functools.partial(expand_quarters_on, bus_axis="head")
 
 
 def layer_norm(values, gain):
@@ -98,7 +107,7 @@
     attn_part = jnp.einsum(
         "hrqd,hde->rqe", attended, out_split, preferred_element_type=jnp.float32
     ).reshape(rows_dev, w_out.shape[1])
-    attn_total = lax.psum(attn_part.astype(jnp.bfloat16), "head").astype(jnp.float32)
+    attn_total = solve_inputs(attn_part.astype(jnp.bfloat16)).astype(jnp.float32)
     hidden_one = layer_norm(tokens.astype(jnp.float32) + attn_total, gain_one).astype(jnp.bfloat16)
     inner = jax.nn.gelu(
         jnp.dot(hidden_one, w_up, preferred_element_type=jnp.float32), approximate=False

time: 387 us -> 366 us (0.946)
  waiting for transfers between devices: 185 us -> 163 us
  local copies, waits for them, and re-layouts: 103 us -> 98.9 us
    psum x1 -> x0, waiting for transfers between devices: 61.6 us -> none  [body(): lax.psum(attn_part.astype(jnp.bfloat16), 'head').astype(jnp.float32)]
    all_gather x0 -> x1, waiting for transfers between devices: none -> 39.6 us  [expand_quarters_on(): z1 = lax.all_gather(here_x, axis_name=bus_axis)]
    reduce_sum x0 -> x1, other arithmetic: none -> 4.3 us  [expand_quarters_on(): return jnp.sum(z1, axis=0)]
  transfers between devices with their start and end apart: 5 -> 5, of which waited for: 5 -> 5; matrix products, arithmetic and copies ran while one was open for 19% -> 20% of each run, Pallas kernels for 0% -> 0%
where the time goes in v1:
time: 366 us; the launch traced here: 365 us
  waiting for transfers between devices  163 us (45%)
  local copies, waits for them, and re-layouts  98.9 us (27%)
  blocking collectives  44.3 us (12%)
  matrix products  23.7 us (6%)
  between operations  14.3 us (4%)
  other arithmetic  11.6 us (3%)
  starting transfers between devices  9.38 us (3%)
    psum x1, waiting for transfers between devices, body(): lax.psum(jnp.dot(inner, w_down, preferred_element_type=jnp.float32).astyp...  65.6 us
    all_gather x1, blocking collectives, body(): lax.all_gather(candidates, 'doc', axis=0, tiled=True)  44.3 us
    all_gather x1, waiting for transfers between devices, expand_quarters_on(): z1 = lax.all_gather(here_x, axis_name=bus_axis)  39.6 us
    all_gather x1, waiting for transfers between devices, body(): gathered = lax.all_gather(prompt_cache, 'doc', axis=1, tiled=True)  27 us
    gather x2, local copies, waits for them, and re-layouts, body(): rel_k_rows = rel_both[1][:, index_one]  25 us
    gather x2, local copies, waits for them, and re-layouts, body(): rel_q_rows = rel_both[0][:, index_two]  23.2 us
    all_gather x1, waiting for transfers between devices, body(): lax.all_gather(query_vectors, 'doc', axis=0, tiled=True)  21.1 us
    reshape x2, local copies, waits for them, and re-layouts, body(): cache_all = gathered.reshape(2, groups_all, PLEN, heads_loc, HD)  13.7 us
  transfers between devices with their start and end apart: 5, of which 5 were waited for; matrix products, arithmetic and copies ran while one was open for 20% of the time, Pallas kernels for 0%

profile of v1, /device:TPU:8, one launch (start us, length us, event | category | flops | bytes accessed | tf_op | source)
XLA Modules:
  0.0 365.3 jit_solution(2498960714608404057)
XLA Ops:
  8.2 1.4 copy.182
  10.3 20.3 %gather_fusion.2 = bf16[3072,2,64]{2,1,0:T(2,128)(2,1)} fusion(bf16[2,512,64]{2,0,1:T(2,128)(2,1)S(1)} %copy.193, s32[3072]{0:T(1024)S(1)} %broadcast_clamp_fusion), kind=kCustom, calls=%fused_computation.2 | custom fusion | bytes 1585152 | tf_op jit(solution)/shard_map/gather | solution.py:94
  30.6 2.9 copy.194
  34.4 0.9 copy.188
  35.6 20.3 %gather_fusion.1 = bf16[3072,2,64]{2,1,0:T(2,128)(2,1)} fusion(bf16[2,512,64]{2,0,1:T(2,128)(2,1)S(1)} %copy.189, s32[3072]{0:T(1024)S(1)} %broadcast_clamp_fusion.1), kind=kCustom, calls=%fused_computation.1 | custom fusion | bytes 1585152 | tf_op jit(solution)/shard_map/gather | solution.py:93
  55.9 4.7 %copy.190 = bf16[32,96,2,64]{1,3,0,2:T(8,128)(2,1)} copy(bf16[32,96,2,64]{3,2,1,0:T(2,128)(2,1)} %bitcast.85) | data formatting | bytes 1572864 | tf_op jit(solution)/shard_map/gather | solution.py:93
  61.0 1.0 copy.198
  62.0 2.5 fusion.11
  64.5 27.0 %all-gather.6.cloned.1.call-done = bf16[2,4096,128]{2,1,0:T(8,128)(2,1)} async-done(((bf16[2,128,128]{2,1,0:T(8,128)(2,1)}), bf16[2,4096,128]{2,1,0:T(8,128)(2,1)}) %all-gather.6.cloned.1.call-update) | async-done | bytes 2097168 | tf_op jit(solution)/shard_map/all_gather | solution.py:72
  91.5 8.2 %reshape.600 = bf16[2,64,64,2,64]{4,3,2,1,0:T(2,128)(2,1)} reshape(bf16[2,4096,128]{2,1,0:T(8,128)(2,1)} %all-gather.6.cloned.1.call-done) | data formatting | bytes 4194304 | tf_op jit(solution)/shard_map/reshape | solution.py:85
  99.7 5.4 %copy.186 = bf16[2,64,64,2,64]{4,2,3,1,0:T(8,128)(2,1)} copy(bf16[2,64,64,2,64]{4,3,2,1,0:T(2,128)(2,1)} %reshape.600) | data formatting | bytes 4194304 | tf_op jit(solution)/shard_map/reshape | solution.py:85
  105.2 2.9 gather_fusion
  108.5 0.8 slice_bitcast_fusion.1
  110.4 3.5 fusion.107
  113.9 1.9 copy.196
  117.4 1.3 bitcast_convert_fusion
  118.9 39.6 %all-gather.10.cloned.1.call-done = bf16[3072,1024]{1,0:T(8,128)(2,1)} async-done(((bf16[384,1024]{1,0:T(8,128)(2,1)}), bf16[3072,1024]{1,0:T(8,128)(2,1)}) %all-gather.10.cloned.1.call-update) | async-done | bytes 6291472 | tf_op jit(solution)/shard_map/all_gather | solution.py:16
  158.6 4.3 %reduce_sum.118 = bf16[384,1024]{1,0:T(8,128)(2,1)S(1)} reduce(bf16[8,384,1024]{2,1,0:T(8,128)(2,1)} %bitcast.84, bf16[]{:T(256)} %constant.57.clone.1), dimensions={0}, to_apply=%region_2.0 | reduce | flops 2752512 | bytes 7077890 | tf_op jit(solution)/shard_map/reduce_sum | solution.py:17
  164.0 4.8 %convolution_convert_fusion = bf16[384,1024]{1,0:T(8,128)(2,1)} fusion(bf16[512,1024]{1,0:T(8,128)(2,1)S(1)} %copy-done, bf16[384,1024]{1,0:T(8,128)(2,1)S(1)} %multiply_convert_fusion.1, bf16[1024,512]{1,0:T(8,128)(2,1)} %param.17), kind=kOutput, calls=%fused_computation.20 | convolution fusion | flops 818479104 | bytes 3670016 | tf_op jit(solution)/shard_map/dot_general | solution.py:116
  168.9 65.6 %all-reduce.2.cloned.1.call-done = bf16[384,1024]{1,0:T(8,128)(2,1)} async-done(((bf16[384,1024]{1,0:T(8,128)(2,1)}), bf16[384,1024]{1,0:T(8,128)(2,1)}) %all-reduce.2.cloned.1.call-update) | async-done | bytes 786448 | tf_op jit(solution)/shard_map/psum | solution.py:115
  234.5 1.5 fusion.3
  238.0 44.3 %all-gather.1 = s32[32,12,8]{1,2,0:T(8,128)S(1)} all-gather(s32[1,12,8]{1,2,0:T(8,128)S(1)} %bitcast.97), channel_id=1, replica_groups=mesh['head'=8,'doc'=32] {'doc'}, dimensions={0}, use_global_device_ids=true | all-gather | bytes 12672 | tf_op jit(solution)/shard_map/all_gather | solution.py:135
  282.6 1.2 convert_reduce_fusion
  284.7 10.3 %gather_fusion.5 = bf16[192,256,128]{2,1,0:T(8,128)(2,1)} fusion(bf16[64,256,128]{2,1,0:T(8,128)(2,1)} %param.24, s32[1024]{0:T(1024)S(1)} %pad_clamp_fusion.1), kind=kCustom, calls=%fused_computation.5 | custom fusion | bytes 25166592 | tf_op jit(solution)/shard_map/gather | solution.py:41
  295.0 1.5 gather_fusion.3
  296.8 21.1 %all-gather.8.cloned.1.call-done = bf16[12288,128]{0,1:T(8,128)(2,1)} async-done(((bf16[384,128]{0,1:T(8,128)(2,1)}), bf16[12288,128]{0,1:T(8,128)(2,1)}) %all-gather.8.cloned.1.call-update) | async-done | bytes 3145744 | tf_op jit(solution)/shard_map/all_gather | solution.py:134
  317.9 4.7 %copy.206 = bf16[12288,128]{1,0:T(8,128)(2,1)} copy(bf16[12288,128]{0,1:T(8,128)(2,1)} %all-gather.8.cloned.1.call-done) | data formatting | bytes 6291456 | tf_op jit(solution)/shard_map/all_gather | solution.py:134
  322.7 3.7 %gather_fusion.4 = bf16[192,32,128]{2,1,0:T(8,128)(2,1)S(1)} fusion(bf16[32,12,32,128]{3,2,1,0:T(8,128)(2,1)} %bitcast.83, s32[192]{0:T(256)S(1)} %reshape.565), kind=kCustom, calls=%fused_computation.4 | custom fusion | bytes 3147264 | tf_op jit(solution)/shard_map/gather | solution.py:151
  326.4 9.2 %select_reduce_fusion = f32[192,32]{1,0:T(8,128)S(1)} fusion(pred[192,256]{1,0:T(8,128)(4,1)S(1)} %iota_compare_fusion, bf16[192,32,128]{2,1,0:T(8,128)(2,1)S(1)} %gather_fusion.4, bf16[192,256,128]{2,1,0:T(8,128)(2,1)} %gather_fusion.5), kind=kOutput, calls=%fused_computation.7 | convolution fusion | flops 405792768 | bytes 14229504 | tf_op jit(solution)/shard_map/sqe,sje->sqj/dot_general | solution.py:43
  336.6 9.0 %all-to-all-start = ((f32[32,1,6]{2,1,0:T(1,128)}), f32[32,1,6]{2,1,0:T(1,128)S(1)}, u32[]{:S(2)}, u32[]{:S(2)}) async-start(f32[32,1,6]{2,1,0:T(1,128)} %copy.210), calls=%async_computation | async-start | bytes 32768 | tf_op jit(solution)/shard_map/all_to_all | solution.py:153
  346.4 9.0 %all-to-all-done = f32[32,1,6]{2,1,0:T(1,128)S(1)} async-done(((f32[32,1,6]{2,1,0:T(1,128)}), f32[32,1,6]{2,1,0:T(1,128)S(1)}, u32[]{:S(2)}, u32[]{:S(2)}) %all-to-all-start) | async-done | bytes 800 | tf_op jit(solution)/shard_map/all_to_all | solution.py:153
  356.7 1.3 gather_fusion.6
  (117 shorter events, 14.7 us)
Async XLA Ops:
  7.2 156.8 %copy-start = (bf16[512,1024]{1,0:T(8,128)(2,1)S(1)}, bf16[512,1024]{1,0:T(8,128)(2,1)}, u32[]{:S(2)}) copy-start(bf16[512,1024]{1,0:T(8,128)(2,1)} %param.18) | copy-start | bytes 3145732
  7.2 2.5 copy-start.9
  7.2 84.3 %all-gather.6.cloned.1.call-start = ((), (), s32[]{:S(2)}) async-start(), calls=%async_computation.1 | async-start | bytes 2162688 | tf_op jit(solution)/shard_map/all_gather | solution.py:72
  7.9 150.6 %all-gather.10.cloned.1.call-start = ((), (), s32[]{:S(2)}) async-start(), calls=%async_computation.4 | async-start | bytes 7077888 | tf_op jit(solution)/shard_map/all_gather | solution.py:16
  30.6 2.9 copy-start.3
  55.9 6.1 %copy-start.18 = (s32[12]{0:T(128)S(1)}, s32[12]{0:T(128)}, u32[]{:S(2)}) copy-start(s32[12]{0:T(128)} %param.26) | copy-start | bytes 148
  60.8 38.9 %copy-start.5 = (bf16[1,2,384,64]{3,2,1,0:T(8,128)(2,1)}, bf16[1,2,384,64]{3,2,1,0:T(8,128)(2,1)S(1)}, u32[]{:S(2)}) copy-start(bf16[1,2,384,64]{3,2,1,0:T(8,128)(2,1)S(1)} %copy.183) | copy-start | bytes 294916
  108.5 1.1 copy-start.8
  113.9 1.9 copy-start.6
  113.9 1.9 copy-start.7
  115.8 1.0 copy-start.11
  115.8 1.1 copy-start.12
  116.2 1.2 copy-start.13
  118.7 115.8 %all-reduce.2.cloned.1.call-start = ((), (), s32[]{:S(2)}) async-start(), calls=%async_computation.2 | async-start | bytes 1572864 | tf_op jit(solution)/shard_map/psum | solution.py:115
  162.9 0.7 copy-start.15
  168.8 67.6 %copy-start.16 = (bf16[1024,128]{1,0:T(8,128)(2,1)S(1)}, bf16[1024,128]{1,0:T(8,128)(2,1)}, u32[]{:S(2)}) copy-start(bf16[1024,128]{1,0:T(8,128)(2,1)} %param.23) | copy-start | bytes 786436
  168.8 67.6 %copy-start.17 = (f32[1024]{0:T(1024)S(1)}, f32[1024]{0:T(1024)}, u32[]{:S(2)}) copy-start(f32[1024]{0:T(1024)} %param.20) | copy-start | bytes 12292
  168.8 149.1 %all-gather.8.cloned.1.call-start = ((), (), s32[]{:S(2)}) async-start(), calls=%async_computation.3 | async-start | bytes 3244032 | tf_op jit(solution)/shard_map/all_gather | solution.py:134
  234.5 1.5 copy-start.4
  236.4 1.3 copy-start.14
  284.7 10.3 %copy-start.2 = (s32[64]{0:T(128)S(1)}, s32[64]{0:T(128)}, u32[]{:S(2)}) copy-start(s32[64]{0:T(128)} %param.25) | copy-start | bytes 772
  326.4 19.3 %copy-start.10 = (bf16[384,128]{0,1:T(8,128)(2,1)S(1)}, bf16[384,128]{0,1:T(8,128)(2,1)}, u32[]{:S(2)}) copy-start(bf16[384,128]{0,1:T(8,128)(2,1)} %multiply_convert_fusion.3) | copy-start | bytes 294916
  326.4 32.4 %copy-start.1 = (bf16[512,1024]{1,0:T(8,128)(2,1)S(1)}, bf16[512,1024]{1,0:T(8,128)(2,1)}, u32[]{:S(2)}) copy-start(bf16[512,1024]{1,0:T(8,128)(2,1)} %param.18) | copy-start | bytes 3145732
  336.6 18.8 %all-to-all-start = ((f32[32,1,6]{2,1,0:T(1,128)}), f32[32,1,6]{2,1,0:T(1,128)S(1)}, u32[]{:S(2)}, u32[]{:S(2)}) async-start(f32[32,1,6]{2,1,0:T(1,128)} %copy.210), calls=%async_computation | async-start | bytes 32768 | tf_op jit(solution)/shard_map/all_to_all | solution.py:153
Sparse Core Ops, SparseCore 0:
  10.6 80.8 all-gather.5
  118.8 39.7 all-gather.9
  168.9 65.5 all-reduce.1
  237.8 80.0 all-gather.7
